TPU v7x, 256 devices: a whole 4x4x8 slice. The times are simulated.
256 devices in a mesh: cfg: 2 (over x_lo), seq: 128 (over y, z, x_hi, core).
Axes of the slice: x: 4 (x_hi: 2, x_lo: 2; x = x_hi * 2 + x_lo), y: 4, z: 8, core: 2. Of those that a mesh axis runs over, the one named last changes fastest.
Arguments:
- queries: bfloat16 [2, 4608, 1536], P('cfg', 'seq'), may hold values from -25 to 25
- keys: bfloat16 [2, 4608, 1536], P('cfg', 'seq'), may hold values from -25 to 25
- values: bfloat16 [2, 4608, 1536], P('cfg', 'seq'), may hold values from -6 to 6
- residual: bfloat16 [2, 4608, 3072], P('cfg', 'seq'), may hold values from -4 to 4
- gate: float32 [2, 3072], P('cfg'), may hold values from 0.5 to 4
- text_len: int32 [2], P('cfg'), may hold values from 64 to 512
- w_out: bfloat16 [1536, 3072], replicated, may hold values from -0.15625 to 0.15625
- w_final: bfloat16 [3072, 64], replicated, may hold values from -0.109375 to 0.109375
- latent: float32 [128, 2048], P('seq', 'cfg'), may hold values from -6 to 6
- owner: int32 [128], replicated, may hold values from 0 to 127, as said below
Outputs:
- hidden_out: bfloat16 [2, 4608, 3072], P('cfg', 'seq')
- latent_next: float32 [128, 2048], P('seq', 'cfg')
Inputs may be any that keep to these rules, and one draw needn't show every extreme that they name: `owner`: a permutation of the indices of seq.
All inputs are finite; a program needn't handle non-finite values.
Results may differ from a plain program's by a relative error of at most 0.0065.
Values may be sent and summed in bfloat16 or wider, within the bound.
A program may use at most 192 MiB of HBM per device.

v0:
```python
import jax
import jax.numpy as jnp
from jax import lax
from jax.sharding import PartitionSpec as P

HEADS = 12
HEAD = 128
CH = 64


def partner_2(x, axis, distance):
    return lax.ppermute(x, axis, [(i, i ^ 1 << distance) for i in range(lax.axis_size(axis))])


def local(queries, keys, values, residual, gate, text_len, w_out, w_final, latent, owner):
    qloc = queries[0]
    kloc = keys[0]
    vloc = values[0]
    tokens, width = qloc.shape
    nseq = lax.axis_size("seq")
    myself = lax.axis_index("seq")
    seqlen = tokens * nseq
    textslots = seqlen // 9
    limit = text_len[0]
    scale = HEAD ** (-0.5)
    both = lax.all_gather(jnp.concatenate([kloc, vloc], axis=1), "seq", axis=0, tiled=True)
    qheads = qloc.reshape(tokens, HEADS, HEAD)
    kall = both[:, :width].reshape(seqlen, HEADS, HEAD)
    vall = both[:, width:].reshape(seqlen, HEADS, HEAD)
    keypos = jnp.arange(seqlen, dtype=jnp.int32)
    valid = (keypos >= textslots) | (keypos < limit)
    scores = jnp.einsum("qhd,khd->hqk", qheads, kall, preferred_element_type=jnp.float32) * scale
    scores = jnp.where(valid[None, None, :], scores, -1e30)
    top = jnp.max(scores, axis=2, keepdims=True)
    expo = jnp.where(valid[None, None, :], jnp.exp(scores - top), 0.0)
    total = jnp.sum(expo, axis=2, keepdims=True)
    accum = jnp.einsum(
        "hqk,khd->hqd", expo.astype(jnp.bfloat16), vall, preferred_element_type=jnp.float32
    )
    attn = (accum / total).astype(jnp.bfloat16).transpose(1, 0, 2).reshape(tokens, width)
    proj = jnp.dot(attn, w_out, preferred_element_type=jnp.float32)
    stream = (residual[0].astype(jnp.float32) + gate[0][None, :] * proj).astype(jnp.bfloat16)
    is_cond = lax.axis_index("cfg") == 0
    speed = jnp.dot(stream, w_final, preferred_element_type=jnp.float32)
    other = partner_2(speed, "cfg", 0)
    speed_cond = jnp.where(is_cond, speed, other)
    speed_free = jnp.where(is_cond, other, speed)
    guided = speed_free + 3.0 * (speed_cond - speed_free)
    gathered = lax.all_gather(guided, "seq", axis=0, tiled=True)
    columns = latent.shape[1]
    tilerows = columns * lax.axis_size("cfg") // CH
    mytile = jnp.sum(jnp.where(owner == myself, jnp.arange(nseq, dtype=jnp.int32), 0))
    picked = lax.dynamic_slice_in_dim(gathered, textslots + mytile * tilerows, tilerows, 0)
    flat = picked.reshape(tilerows * CH)
    mine = lax.dynamic_slice_in_dim(flat, lax.axis_index("cfg") * columns, columns, 0)
    latent_next = latent - 0.25 * mine.reshape(1, columns)
    return (stream[None], latent_next)


def solution(mesh):
    placed = (
        P("cfg", "seq", None),
        P("cfg", "seq", None),
        P("cfg", "seq", None),
        P("cfg", "seq", None),
        P("cfg", None),
        P("cfg"),
        P(),
        P(),
        P("seq", "cfg"),
        P(),
    )
    return jax.shard_map(
        local,
        mesh=mesh,
        in_specs=placed,
        out_specs=(P("cfg", "seq", None), P("seq", "cfg")),
        check_vma=False,
    )
```

profile of v0, /device:TPU:1, one launch (start us, length us, event | category | flops | bytes accessed | tf_op | source)
XLA Modules:
  0.0 468.3 jit_solution(7332716834692380684)
XLA Ops:
  7.2 0.0 all-gather.5.cloned.1.call-start
  7.2 1.7 maximum_bitcast_fusion
  8.9 0.0 all-gather.5.cloned.1.call-update
  9.0 0.0 all-gather.7.cloned.1.call-start
  9.7 1.0 reshape_squeeze.3
  10.7 210.0 %all-gather.5.cloned.1.call-done = bf16[128,36,3072]{2,1,0:T(8,128)(2,1)} async-done(((bf16[1,36,3072]{2,1,0:T(8,128)(2,1)}), bf16[128,36,3072]{2,1,0:T(8,128)(2,1)}) %all-gather.5.cloned.1.call-update) | async-done | bytes 28311568 | tf_op jit(solution)/shard_map/all_gather | solution.py:26
  220.7 33.4 %reshape.35 = bf16[4608,3072]{1,0:T(8,128)(2,1)} reshape(bf16[128,36,3072]{2,1,0:T(8,128)(2,1)} %all-gather.5.cloned.1.call-done) | data formatting | bytes 56623104
  254.1 20.7 %fusion.21 = (bf16[4608,1536]{1,0:T(8,128)(2,1)}, bf16[4608,1536]{1,0:T(8,128)(2,1)}) fusion(bf16[4608,3072]{1,0:T(8,128)(2,1)} %reshape.35), kind=kLoop, calls=%fused_computation.24 | loop fusion | bytes 56623104 | tf_op jit(solution)/shard_map/slice | solution.py:28
  274.7 18.8 %copy.19 = bf16[4608,1536]{0,1:T(8,128)(2,1)} copy(bf16[4608,1536]{1,0:T(8,128)(2,1)} %get-tuple-element.2) | data formatting | bytes 28311552 | tf_op jit(solution)/shard_map/slice | solution.py:28
  293.5 6.2 %multiply_select_fusion = f32[12,4608,36]{1,2,0:T(8,128)S(1)} fusion(bf16[4608,12,128]{0,2,1:T(8,128)(2,1)} %bitcast.41, pred[4608]{0:T(1024)(128)(4,1)S(1)} %fusion.19, bf16[36,12,128]{2,1,0:T(8,128)(2,1)S(1)} %reshape_squeeze.3), kind=kOutput, calls=%fused_computation.5 | convolution fusion | flops 513589248 | bytes 22233600 | tf_op jit(solution)/shard_map/qhd,khd->hqk/dot_general | solution.py:32
  299.7 4.8 %fusion.22 = (f32[12,36]{1,0:T(8,128)S(1)}, bf16[12,36,4608]{2,1,0:T(8,128)(2,1)}) fusion(f32[12,4608,36]{1,2,0:T(8,128)S(1)} %multiply_select_fusion, pred[4608]{0:T(1024)(128)(4,1)S(1)} %fusion.19), kind=kOutput, calls=%fused_computation.25 | output fusion | flops 7967231 | bytes 11950272 | tf_op jit(solution)/shard_map/sub | solution.py:35
  304.5 18.5 %copy.22 = bf16[4608,1536]{0,1:T(8,128)(2,1)} copy(bf16[4608,1536]{1,0:T(8,128)(2,1)} %get-tuple-element.3) | data formatting | bytes 28311552 | tf_op jit(solution)/shard_map/slice | solution.py:29
  323.0 11.1 %fusion.15 = bf16[36,12,128]{2,0,1:T(8,128)(2,1)S(1)} fusion(bf16[4608,12,128]{0,2,1:T(8,128)(2,1)} %bitcast.42, bf16[12,36,4608]{2,1,0:T(8,128)(2,1)} %get-tuple-element.5, f32[36,12]{0,1:T(8,128)S(1)} %bitcast.50), kind=kOutput, calls=%fused_computation.13 | convolution fusion | flops 509718528 | bytes 18249408 | tf_op jit(solution)/shard_map/hqk,khd->hqd/dot_general | solution.py:37
  334.3 5.4 %fusion.8 = bf16[36,3072]{1,0:T(8,128)(2,1)S(1)} fusion(bf16[36,1536]{1,0:T(8,128)(2,1)S(1)} %bitcast.44, bf16[1536,3072]{1,0:T(8,128)(2,1)} %param.16, bf16[1,36,3072]{2,1,0:T(8,128)(2,1)S(1)} %copy-done.2, f32[3072]{0:T(1024)S(1)} %bitcast.49), kind=kOutput, calls=%fused_computation.10 | convolution fusion | flops 340180992 | bytes 10002432 | tf_op jit(solution)/shard_map/dot_general | solution.py:41
  339.7 0.2 fusion.23
  340.0 0.3 collective-permute-start
  340.3 2.4 collective-permute-done
  342.7 0.6 add_bitcast_fusion
  343.3 0.0 all-gather.7.cloned.1.call-update
  343.3 0.6 fusion.20
  344.6 113.7 %all-gather.7.cloned.1.call-done = f32[128,36,64]{2,1,0:T(8,128)} async-done(((f32[1,36,64]{2,1,0:T(8,128)}), f32[128,36,64]{2,1,0:T(8,128)}) %all-gather.7.cloned.1.call-update) | async-done | bytes 1179664 | tf_op jit(solution)/shard_map/all_gather | solution.py:49
  458.3 2.4 reshape.37
  460.7 0.1 reshape.32
  460.8 0.6 sub.17
  (18 shorter events, 0.2 us)
Async XLA Ops:
  7.2 332.6 %copy-start = (bf16[3072,64]{0,1:T(8,128)(2,1)S(1)}, bf16[3072,64]{0,1:T(8,128)(2,1)}, u32[]{:S(2)}) copy-start(bf16[3072,64]{0,1:T(8,128)(2,1)} %param.17) | copy-start | bytes 1179652
  7.2 213.5 %all-gather.5.cloned.1.call-start = ((), (), s32[]{:S(2)}) async-start(), calls=%async_computation | async-start | bytes 31703040 | tf_op jit(solution)/shard_map/all_gather | solution.py:26
  9.0 449.3 %all-gather.7.cloned.1.call-start = ((), (), s32[]{:S(2)}) async-start(), calls=%async_computation.1 | async-start | bytes 2641920 | tf_op jit(solution)/shard_map/all_gather | solution.py:49
  323.0 11.2 %copy-start.2 = (bf16[1,36,3072]{2,1,0:T(8,128)(2,1)S(1)}, bf16[1,36,3072]{2,1,0:T(8,128)(2,1)}, u32[]{:S(2)}) copy-start(bf16[1,36,3072]{2,1,0:T(8,128)(2,1)} %param.13) | copy-start | bytes 663556
  323.0 11.2 %copy-start.3 = (f32[1,3072]{1,0:T(1,128)S(1)}, f32[1,3072]{1,0:T(1,128)}, u32[]{:S(2)}) copy-start(f32[1,3072]{1,0:T(1,128)} %param.14) | copy-start | bytes 36868
  334.2 9.1 %copy-start.5 = (s32[128]{0:T(128)S(1)}, s32[128]{0:T(128)}, u32[]{:S(2)}) copy-start(s32[128]{0:T(128)} %param.19) | copy-start | bytes 1540
  334.3 126.5 %copy-start.4 = (f32[1,1024]{1,0:T(1,128)S(1)}, f32[1,1024]{1,0:T(1,128)}, u32[]{:S(2)}) copy-start(f32[1,1024]{1,0:T(1,128)} %param.18) | copy-start | bytes 12292
  339.7 121.7 %copy-start.1 = (bf16[36,3072]{1,0:T(8,128)(2,1)}, bf16[36,3072]{1,0:T(8,128)(2,1)S(1)}, u32[]{:S(2)}) copy-start(bf16[36,3072]{1,0:T(8,128)(2,1)S(1)} %fusion.8) | copy-start | bytes 663556
  340.0 2.7 collective-permute-start
Sparse Core Ops, SparseCore 0:
  12.4 208.1 all-gather.4
  343.4 114.8 all-gather.6
where the time goes:
time: 470 us; the launch traced here: 468 us
  waiting for transfers between devices  326 us (69%)
  local copies, waits for them, and re-layouts  95 us (20%)
  matrix products  22.9 us (5%)
  between operations  15.5 us (3%)
  other arithmetic  8.35 us (2%)
    all_gather x1, waiting for transfers between devices, local(): lax.all_gather(jnp.concatenate([kloc, vloc], axis=1), 'seq', axis=0, tile...  210 us
    all_gather x1, waiting for transfers between devices, local(): gathered = lax.all_gather(guided, 'seq', axis=0, tiled=True)  114 us
    slice x2, local copies, waits for them, and re-layouts, local(): kall = both[:, :width].reshape(seqlen, HEADS, HEAD)  39.4 us
    unnamed x16, local copies, waits for them, and re-layouts  35.9 us
    slice x1, local copies, waits for them, and re-layouts, local(): vall = both[:, width:].reshape(seqlen, HEADS, HEAD)  18.5 us
    dot_general x1, matrix products, local(): jnp.einsum('hqk,khd->hqd', expo.astype(jnp.bfloat16), vall, preferred_ele...  11.1 us
  transfers between devices with their start and end apart: 3, of which 3 were waited for; matrix products, arithmetic and copies ran while one was open for 0% of the time, Pallas kernels for 0%

commit v1 on v0

--- a/solution.py
+++ b/solution.py
@@ -1,3 +1,4 @@
+import functools
 import jax
 import jax.numpy as jnp
 from jax import lax
@@ -6,6 +7,15 @@
 HEADS = 12
 HEAD = 128
 CH = 64
+
+
+def move_scales(original, net_axis):
+    arr_next = jnp.stack([original for _ in range(jax.lax.axis_size(net_axis))], 0)
+    before = jax.lax.all_to_all(arr_next, net_axis, 0, 0)
+    return jnp.concatenate(before, 0)
+
+
+_follow_heads = functools.partial(move_scales, net_axis="seq")
 
 
 def partner_2(x, axis, distance):
@@ -23,7 +33,7 @@
     textslots = seqlen // 9
     limit = text_len[0]
     scale = HEAD ** (-0.5)
-    both = lax.all_gather(jnp.concatenate([kloc, vloc], axis=1), "seq", axis=0, tiled=True)
+    both = _follow_heads(jnp.concatenate([kloc, vloc], axis=1))
     qheads = qloc.reshape(tokens, HEADS, HEAD)
     kall = both[:, :width].reshape(seqlen, HEADS, HEAD)
     vall = both[:, width:].reshape(seqlen, HEADS, HEAD)

time: 470 us -> 989 us (2.10)
  waiting for transfers between devices: 326 us -> 819 us
  starting transfers between devices: 0.41 us -> 17 us
  local copies, waits for them, and re-layouts: 95 us -> 105 us
    all_to_all x0 -> x1, waiting for transfers between devices: none -> 683 us  [move_scales(): before = jax.lax.all_to_all(arr_next, net_axis, 0, 0)]
    all_gather x1 -> x0, waiting for transfers between devices: 210 us -> none  [local(): lax.all_gather(jnp.concatenate([kloc, vloc], axis=1), 'seq', axis=0, tile...]
    reshape x0 -> x1, local copies, waits for them, and re-layouts: none -> 33.4 us  [move_scales(): return jnp.concatenate(before, 0)]
    unnamed x16 -> x17, local copies, waits for them, and re-layouts: 35.9 us -> 2.54 us
    all_gather x1, waiting for transfers between devices: 114 us -> 133 us  [local(): gathered = lax.all_gather(guided, 'seq', axis=0, tiled=True)]
    all_to_all x0 -> x1, starting transfers between devices: none -> 16.9 us  [move_scales(): before = jax.lax.all_to_all(arr_next, net_axis, 0, 0)]
    another operation x0 -> x1, local copies, waits for them, and re-layouts: none -> 10.6 us  [move_scales(): jnp.stack([original for _ in range(jax.lax.axis_size(net_axis))], 0)]
where the time goes in v1:
time: 989 us; the launch traced here: 987 us
  waiting for transfers between devices  819 us (83%)
  local copies, waits for them, and re-layouts  105 us (11%)
  matrix products  22.9 us (2%)
  starting transfers between devices  17 us (2%)
  between operations  15.5 us (2%)
    all_to_all x1, waiting for transfers between devices, move_scales(): before = jax.lax.all_to_all(arr_next, net_axis, 0, 0)  683 us
    all_gather x1, waiting for transfers between devices, local(): gathered = lax.all_gather(guided, 'seq', axis=0, tiled=True)  133 us
    slice x2, local copies, waits for them, and re-layouts, local(): kall = both[:, :width].reshape(seqlen, HEADS, HEAD)  39.4 us
    reshape x1, local copies, waits for them, and re-layouts, move_scales(): return jnp.concatenate(before, 0)  33.4 us
  transfers between devices with their start and end apart: 3, of which 3 were waited for; matrix products, arithmetic and copies ran while one was open for 0% of the time, Pallas kernels for 0%

profile of v1, /device:TPU:1, one launch (start us, length us, event | category | flops | bytes accessed | tf_op | source)
XLA Modules:
  0.0 986.7 jit_solution(7105391379180451074)
XLA Ops:
  7.2 1.0 pad_maximum_fusion
  8.2 10.6 %stack.2 = bf16[128,36,3072]{2,1,0:T(8,128)(2,1)} broadcast(bf16[36,3072]{1,0:T(8,128)(2,1)S(1)} %pad_maximum_fusion), dimensions={1,2} | broadcast | bytes 28532736 | tf_op jit(solution)/shard_map/stack | solution.py:13
  18.8 16.9 %all-to-all-start = ((bf16[128,36,3072]{2,1,0:T(8,128)(2,1)}), bf16[128,36,3072]{2,1,0:T(8,128)(2,1)}, u32[]{:S(2)}, u32[]{:S(2)}) async-start(bf16[128,36,3072]{2,1,0:T(8,128)(2,1)} %stack.2), calls=%async_computation | async-start | bytes 62914560 | tf_op jit(solution)/shard_map/all_to_all | solution.py:14
  35.7 0.0 all-gather.3.cloned.1.call-start
  36.4 0.1 reshape_squeeze.3
  36.5 682.8 %all-to-all-done = bf16[128,36,3072]{2,1,0:T(8,128)(2,1)} async-done(((bf16[128,36,3072]{2,1,0:T(8,128)(2,1)}), bf16[128,36,3072]{2,1,0:T(8,128)(2,1)}, u32[]{:S(2)}, u32[]{:S(2)}) %all-to-all-start) | async-done | bytes 28311584 | tf_op jit(solution)/shard_map/all_to_all | solution.py:14
  719.3 33.4 %reshape.34 = bf16[4608,3072]{1,0:T(8,128)(2,1)} reshape(bf16[128,36,3072]{2,1,0:T(8,128)(2,1)} %all-to-all-done) | data formatting | bytes 56623104 | tf_op jit(solution)/shard_map/reshape | solution.py:15
  752.7 20.7 %fusion.21 = (bf16[4608,1536]{1,0:T(8,128)(2,1)}, bf16[4608,1536]{1,0:T(8,128)(2,1)}) fusion(bf16[4608,3072]{1,0:T(8,128)(2,1)} %reshape.34), kind=kLoop, calls=%fused_computation.24 | loop fusion | bytes 56623104 | tf_op jit(solution)/shard_map/slice | solution.py:38
  773.4 18.8 %copy.19 = bf16[4608,1536]{0,1:T(8,128)(2,1)} copy(bf16[4608,1536]{1,0:T(8,128)(2,1)} %get-tuple-element.2) | data formatting | bytes 28311552 | tf_op jit(solution)/shard_map/slice | solution.py:38
  792.1 6.2 multiply_select_fusion
  798.3 4.8 fusion.22
  803.1 18.5 %copy.22 = bf16[4608,1536]{0,1:T(8,128)(2,1)} copy(bf16[4608,1536]{1,0:T(8,128)(2,1)} %get-tuple-element.3) | data formatting | bytes 28311552 | tf_op jit(solution)/shard_map/slice | solution.py:39
  821.7 11.1 %fusion.15 = bf16[36,12,128]{2,0,1:T(8,128)(2,1)S(1)} fusion(bf16[4608,12,128]{0,2,1:T(8,128)(2,1)} %bitcast.40, bf16[12,36,4608]{2,1,0:T(8,128)(2,1)} %get-tuple-element.5, f32[36,12]{0,1:T(8,128)S(1)} %bitcast.48), kind=kOutput, calls=%fused_computation.13 | convolution fusion | flops 509718528 | bytes 18249408 | tf_op jit(solution)/shard_map/hqk,khd->hqd/dot_general | solution.py:47
  832.9 5.4 fusion.8
  838.4 0.2 fusion.23
  838.6 0.1 collective-permute-start
  838.7 2.6 collective-permute-done
  841.3 0.6 add_bitcast_fusion
  841.9 0.0 all-gather.3.cloned.1.call-update
  841.9 0.6 fusion.20
  843.2 133.5 %all-gather.3.cloned.1.call-done = f32[128,36,64]{2,1,0:T(8,128)} async-done(((f32[1,36,64]{2,1,0:T(8,128)}), f32[128,36,64]{2,1,0:T(8,128)}) %all-gather.3.cloned.1.call-update) | async-done | bytes 1179664 | tf_op jit(solution)/shard_map/all_gather | solution.py:59
  976.7 2.4 reshape.41
  979.2 0.1 reshape.38
  979.3 0.6 sub.17
  (20 shorter events, 0.2 us)
Async XLA Ops:
  7.2 831.2 %copy-start = (bf16[3072,64]{0,1:T(8,128)(2,1)S(1)}, bf16[3072,64]{0,1:T(8,128)(2,1)}, u32[]{:S(2)}) copy-start(bf16[3072,64]{0,1:T(8,128)(2,1)} %param.17) | copy-start | bytes 1179652
  18.8 17.6 %copy-start.3 = (bf16[1,36,1536]{2,1,0:T(8,128)(2,1)S(1)}, bf16[1,36,1536]{2,1,0:T(8,128)(2,1)}, u32[]{:S(2)}) copy-start(bf16[1,36,1536]{2,1,0:T(8,128)(2,1)} %param.10) | copy-start | bytes 331780
  18.8 700.5 %all-to-all-start = ((bf16[128,36,3072]{2,1,0:T(8,128)(2,1)}), bf16[128,36,3072]{2,1,0:T(8,128)(2,1)}, u32[]{:S(2)}, u32[]{:S(2)}) async-start(bf16[128,36,3072]{2,1,0:T(8,128)(2,1)} %stack.2), calls=%async_computation | async-start | bytes 62914560 | tf_op jit(solution)/shard_map/all_to_all | solution.py:14
  35.7 941.0 %all-gather.3.cloned.1.call-start = ((), (), s32[]{:S(2)}) async-start(), calls=%async_computation.1 | async-start | bytes 2641920 | tf_op jit(solution)/shard_map/all_gather | solution.py:59
  821.7 11.2 %copy-start.2 = (bf16[1,36,3072]{2,1,0:T(8,128)(2,1)S(1)}, bf16[1,36,3072]{2,1,0:T(8,128)(2,1)}, u32[]{:S(2)}) copy-start(bf16[1,36,3072]{2,1,0:T(8,128)(2,1)} %param.13) | copy-start | bytes 663556
  821.7 11.2 %copy-start.4 = (f32[1,3072]{1,0:T(1,128)S(1)}, f32[1,3072]{1,0:T(1,128)}, u32[]{:S(2)}) copy-start(f32[1,3072]{1,0:T(1,128)} %param.14) | copy-start | bytes 36868
  832.8 9.1 copy-start.6
  832.9 146.3 %copy-start.5 = (f32[1,1024]{1,0:T(1,128)S(1)}, f32[1,1024]{1,0:T(1,128)}, u32[]{:S(2)}) copy-start(f32[1,1024]{1,0:T(1,128)} %param.18) | copy-start | bytes 12292
  838.4 141.5 %copy-start.1 = (bf16[36,3072]{1,0:T(8,128)(2,1)}, bf16[36,3072]{1,0:T(8,128)(2,1)S(1)}, u32[]{:S(2)}) copy-start(bf16[36,3072]{1,0:T(8,128)(2,1)S(1)} %fusion.8) | copy-start | bytes 663556
  838.6 2.7 collective-permute-start
Sparse Core Ops, SparseCore 0:
  842.1 134.6 all-gather.2
